TPU v7x, 512 devices: a whole 4x4x16 slice. The times are simulated.
512 devices in a mesh: ctx: 64 (over z, x_hi, core), head: 8 (over x_lo, y).
Axes of the slice: x: 4 (x_hi: 2, x_lo: 2; x = x_hi * 2 + x_lo), y: 4, z: 16, core: 2. Of those that a mesh axis runs over, the one named last changes fastest.
Arguments:
- queries: bfloat16 [16384, 4096], P('ctx', 'head'), may hold values from -6 to 6
- key_rows: bfloat16 [16384, 1024], P('ctx', 'head'), may hold values from -6 to 6
- value_rows: bfloat16 [16384, 1024], P('ctx', 'head'), may hold values from -6 to 6
- attn_out: bfloat16 [16384, 4096], P('ctx', 'head'), may hold values from -6 to 6
- out_grad: bfloat16 [16384, 4096], P('ctx', 'head'), may hold values from -6 to 6
- log_sums: float32 [32, 16384], P('head', 'ctx'), may hold values from 4.5 to 6
- block_picks: int32 [128, 32, 3], P('ctx', 'head'), may hold values from 0 to 3, all different within a row
- query_weight: bfloat16 [4096, 4096], P('ctx', 'head'), may hold values from -0.21875 to 0.21875
- key_weight: bfloat16 [4096, 1024], P('ctx', 'head'), may hold values from -0.21875 to 0.21875
- value_weight: bfloat16 [4096, 1024], P('ctx', 'head'), may hold values from -0.21875 to 0.21875
Outputs:
- input_grad: bfloat16 [16384, 4096], P('ctx', 'head')
Inputs may be any that keep to these rules, and one draw needn't show every extreme that they name: `block_picks`: in each row (query block, query head) the 3 entries differ; entry m selects the block m + 1 blocks before the query's block, and selections before the sequence's start select nothing.
All inputs are finite; a program needn't handle non-finite values.
Results may differ from a plain program's by a relative error of at most 0.013.
Values may be sent and summed in bfloat16 or wider, within the bound.
No kernel may reach another device: no remote copies, remote signals or barrier semaphores. Data moves between devices by JAX's collectives and lax.ppermute only.
A program may use at most 64 MiB of HBM per device.

v0:
```python
import math
import jax
import jax.numpy as jnp
from jax import lax
from jax.sharding import PartitionSpec as P

BLK = 128


def passed_along(x, axis, by):
    devices = lax.axis_size(axis)
    pairs = [(i, i + by) for i in range(devices) if 0 <= i + by < devices]
    return lax.ppermute(x, axis, pairs)


def block_grads(
    query_blocks,
    grad_blocks,
    log_part,
    delta_part,
    pick_part,
    query_first,
    key_table,
    value_table,
    key_first,
):
    blocks, width, group, head_dim = query_blocks.shape
    table_blocks = key_table.shape[0]
    scaling = 1.0 / math.sqrt(head_dim)
    offsets = jnp.concatenate([jnp.zeros((blocks, group, 1), jnp.int32), pick_part + 1], axis=2)
    query_ids = query_first + jnp.arange(blocks, dtype=jnp.int32)
    key_block = query_ids[:, None, None] - offsets
    table_index = key_block - key_first
    usable = (table_index >= 0) & (table_index < table_blocks) & (key_block >= 0)
    clipped = jnp.clip(table_index, 0, table_blocks - 1)
    key_sel = key_table[clipped]
    value_sel = value_table[clipped]
    scores = (
        jnp.einsum("bqgd,bgskd->bgqsk", query_blocks, key_sel, preferred_element_type=jnp.float32)
        * scaling
    )
    position = jnp.arange(width)
    causal = position[:, None] >= position[None, :]
    allowed = usable[:, :, None, :, None] & (
        (offsets != 0)[:, :, None, :, None] | causal[None, None, :, None, :]
    )
    probability = jnp.where(allowed, jnp.exp(scores - log_part[:, :, :, None, None]), 0.0)
    prob_grad = jnp.einsum(
        "bqgd,bgskd->bgqsk", grad_blocks, value_sel, preferred_element_type=jnp.float32
    )
    score_grad = probability * (prob_grad - delta_part[:, :, :, None, None])
    prob_half = probability.astype(jnp.bfloat16)
    grad_half = score_grad.astype(jnp.bfloat16)
    query_grad = (
        jnp.einsum("bgqsk,bgskd->bqgd", grad_half, key_sel, preferred_element_type=jnp.float32)
        * scaling
    )
    key_terms = (
        jnp.einsum("bgqsk,bqgd->bgskd", grad_half, query_blocks, preferred_element_type=jnp.float32)
        * scaling
    )
    value_terms = jnp.einsum(
        "bgqsk,bqgd->bgskd", prob_half, grad_blocks, preferred_element_type=jnp.float32
    )
    onehot = (usable[..., None] & (clipped[..., None] == jnp.arange(table_blocks))).astype(
        jnp.float32
    )
    key_grad = jnp.einsum("bgsc,bgskd->ckd", onehot, key_terms, precision=lax.Precision.HIGHEST)
    value_grad = jnp.einsum("bgsc,bgskd->ckd", onehot, value_terms, precision=lax.Precision.HIGHEST)
    return (query_grad, key_grad, value_grad)


def per_device(
    queries,
    key_rows,
    value_rows,
    attn_out,
    out_grad,
    log_sums,
    block_picks,
    query_weight,
    key_weight,
    value_weight,
):
    tokens, query_cols = queries.shape
    head_dim = key_rows.shape[1]
    group = query_cols // head_dim
    width = BLK
    blocks = tokens // width
    cycle_pos = lax.axis_index("ctx")
    own_first = cycle_pos * blocks
    query_blocks = queries.reshape(blocks, width, group, head_dim)
    grad_blocks = out_grad.reshape(blocks, width, group, head_dim)
    delta_part = jnp.sum(
        (out_grad.astype(jnp.float32) * attn_out.astype(jnp.float32)).reshape(
            blocks, width, group, head_dim
        ),
        axis=3,
    ).transpose(0, 2, 1)
    log_part = log_sums.reshape(group, blocks, width).transpose(1, 0, 2)
    fetched = []
    for distance in (1, 2):
        fetched.append(passed_along((key_rows, value_rows), "ctx", distance))
    key_table = jnp.concatenate([fetched[1][0], fetched[0][0], key_rows], axis=0).reshape(
        3 * blocks, width, head_dim
    )
    value_table = jnp.concatenate([fetched[1][1], fetched[0][1], value_rows], axis=0).reshape(
        3 * blocks, width, head_dim
    )
    query_grad, key_grad, value_grad = block_grads(
        query_blocks,
        grad_blocks,
        log_part,
        delta_part,
        block_picks,
        own_first,
        key_table,
        value_table,
        own_first - 2 * blocks,
    )
    key_own = key_grad[2 * blocks :]
    value_own = value_grad[2 * blocks :]
    for distance in (1, 2):
        lower = (2 - distance) * blocks
        returned = passed_along(
            (key_grad[lower : lower + blocks], value_grad[lower : lower + blocks]), "ctx", -distance
        )
        key_own = key_own + returned[0]
        value_own = value_own + returned[1]
    grads = jnp.concatenate(
        [
            query_grad.reshape(tokens, query_cols).astype(jnp.bfloat16),
            key_own.reshape(tokens, head_dim).astype(jnp.bfloat16),
            value_own.reshape(tokens, head_dim).astype(jnp.bfloat16),
        ],
        axis=1,
    )
    weight_cat = jnp.concatenate([query_weight, key_weight, value_weight], axis=1)
    partial_value = lax.dot_general(
        grads,
        lax.all_gather(weight_cat, "ctx", axis=0, tiled=True),
        (((1,), (1,)), ((), ())),
        preferred_element_type=jnp.float32,
    )
    return lax.psum_scatter(
        partial_value.astype(jnp.bfloat16), "head", scatter_dimension=1, tiled=True
    )


def solution(mesh):
    placed = (
        P("ctx", "head"),
        P("ctx", "head"),
        P("ctx", "head"),
        P("ctx", "head"),
        P("ctx", "head"),
        P("head", "ctx"),
        P("ctx", "head", None),
        P("ctx", "head"),
        P("ctx", "head"),
        P("ctx", "head"),
    )
    return jax.shard_map(
        per_device, mesh=mesh, in_specs=placed, out_specs=P("ctx", "head"), check_vma=False
    )
```

profile of v0, /device:TPU:4, one launch (start us, length us, event | category | flops | bytes accessed | tf_op | source)
XLA Modules:
  0.0 230.7 jit_solution(6480486702893773419)
XLA Ops:
  6.5 1.5 pad_maximum_fusion.2
  8.1 0.0 all-gather.2.cloned.1.call-update
  8.1 0.0 reduce-scatter.2.cloned.1.call-start
  8.1 3.8 %collective-permute-start = (bf16[256,128]{1,0:T(8,128)(2,1)}, bf16[256,128]{1,0:T(8,128)(2,1)S(1)}, u32[]{:S(2)}, u32[]{:S(2)}) collective-permute-start(bf16[256,128]{1,0:T(8,128)(2,1)} %param.11), channel_id=1, source_target_pairs={{0,16},{8,24},{16,32},{24,40},{32,48},{40,56},{48,64},{56,72},{64,... | collective-permute-start | bytes 196616 | tf_op jit(solution)/shard_map/ppermute | solution.py:13
  11.9 1.9 collective-permute-start.1
  13.8 4.9 %collective-permute-start.2 = (bf16[256,128]{1,0:T(8,128)(2,1)}, bf16[256,128]{1,0:T(8,128)(2,1)S(1)}, u32[]{:S(2)}, u32[]{:S(2)}) collective-permute-start(bf16[256,128]{1,0:T(8,128)(2,1)} %param.12), channel_id=1, source_target_pairs={{0,16},{8,24},{16,32},{24,40},{32,48},{40,56},{48,64},{56,72},{64,... | collective-permute-start | bytes 196616 | tf_op jit(solution)/shard_map/ppermute | solution.py:13
  18.8 3.6 %collective-permute-start.3 = (bf16[256,128]{1,0:T(8,128)(2,1)}, bf16[256,128]{1,0:T(8,128)(2,1)S(1)}, u32[]{:S(2)}, u32[]{:S(2)}) collective-permute-start(bf16[256,128]{1,0:T(8,128)(2,1)} %param.12), channel_id=1, source_target_pairs={{0,8},{8,16},{16,24},{24,32},{32,40},{40,48},{48,56},{56,64},{64,7... | collective-permute-start | bytes 196616 | tf_op jit(solution)/shard_map/ppermute | solution.py:13
  22.4 0.7 broadcast_add_fusion
  23.1 0.1 compare_select_fusion
  23.2 0.1 copy.38
  23.3 0.1 reshape.54
  23.4 0.1 compare_and_fusion
  23.4 0.1 copy.40
  23.6 0.1 copy.41
  23.7 1.0 reshape.47
  24.7 1.0 reshape.50
  25.7 1.1 convert_multiply_fusion
  26.8 0.0 copy-start.1
  26.8 0.2 reshape.51
  27.0 0.3 reduce_sum.9
  27.4 0.1 copy.46
  27.4 0.1 copy.50
  27.6 0.0 collective-permute-done.1
  27.6 0.0 copy-start.2
  27.7 0.7 gather_fusion
  28.5 0.7 gather_fusion.1
  29.2 0.7 bitcast_select_fusion
  30.0 0.5 fusion
  30.4 0.4 convolution_multiply_fusion
  30.9 3.3 %fusion.5 = f32[6,128,128]{2,0,1:T(8,128)S(1)} fusion(f32[2,4,4,128,128]{4,3,2,1,0:T(8,128)S(1)} %convolution_multiply_fusion, s32[2,4,4]{2,1,0:T(4,128)S(1)} %copy.50, pred[2,4,4]{2,1,0:T(4,128)(4,1)S(1)} %copy.40), kind=kOutput, calls=%fused_computation.11 | convolution fusion | flops 37749120 | bytes 2490528 | tf_op jit(solution)/shard_map/bgsc,bgskd->ckd/dot_general | solution.py:68
  34.2 0.1 fusion.34
  34.3 3.5 %collective-permute-start.4 = (f32[2,128,128]{2,0,1:T(2,128)S(1)}, f32[2,128,128]{2,0,1:T(2,128)S(1)}, u32[]{:S(2)}, u32[]{:S(2)}) collective-permute-start(f32[2,128,128]{2,0,1:T(2,128)S(1)} %get-tuple-element.7), channel_id=1, source_target_pairs={{8,0},{16,8},{24,16},{32,24},{40,32},{48,40},{56,48},{64,56},{72,6... | collective-permute-start | bytes 393224 | tf_op jit(solution)/shard_map/ppermute | solution.py:13
  37.8 1.9 collective-permute-start.5
  39.7 0.4 fusion.14
  40.1 3.3 %fusion.8 = f32[6,128,128]{2,0,1:T(8,128)S(1)} fusion(f32[2,4,4,128,128]{4,3,2,1,0:T(8,128)S(1)} %fusion.14, s32[2,4,4]{2,1,0:T(4,128)S(1)} %copy.50, pred[2,4,4]{2,1,0:T(4,128)(4,1)S(1)} %copy.40), kind=kOutput, calls=%fused_computation.12 | convolution fusion | flops 37749120 | bytes 2490528 | tf_op jit(solution)/shard_map/bgsc,bgskd->ckd/dot_general | solution.py:69
  43.4 0.5 fusion.13
  43.9 0.1 fusion.35
  44.0 1.9 collective-permute-start.6
  46.0 1.9 collective-permute-start.7
  47.9 0.2 copy.48
  48.2 0.1 fusion.28
  48.3 0.1 collective-permute-done.6
  48.5 8.6 %collective-permute-done.7 = f32[2,128,128]{2,0,1:T(2,128)S(1)} collective-permute-done((f32[2,128,128]{2,0,1:T(2,128)S(1)}, f32[2,128,128]{2,0,1:T(2,128)S(1)}, u32[]{:S(2)}, u32[]{:S(2)}) %collective-permute-start.7) | collective-permute-done | bytes 131104 | tf_op jit(solution)/shard_map/ppermute | solution.py:13
  57.1 0.1 fusion.26
  57.2 113.4 %all-gather.2.cloned.1.call-done = bf16[4096,768]{1,0:T(8,128)(2,1)} async-done(((bf16[64,768]{1,0:T(8,128)(2,1)}), bf16[4096,768]{1,0:T(8,128)(2,1)}) %all-gather.2.cloned.1.call-update) | async-done | bytes 6291472 | tf_op jit(solution)/shard_map/all_gather | solution.py:141
  170.6 6.0 %convolution_convert_fusion = bf16[256,4096]{1,0:T(8,128)(2,1)} fusion(bf16[4096,768]{1,0:T(8,128)(2,1)} %all-gather.2.cloned.1.call-done, bf16[256,128]{1,0:T(8,128)(2,1)S(1)} %bitcast.71, bf16[256,128]{1,0:T(8,128)(2,1)S(1)} %bitcast.70, bf16[256,512]{1,0:T(8,128)(2,1)S(1)} %bitcast.69), kind=kOutput, calls=%fused_computation.2 | convolution fusion | flops 1612840960 | bytes 8781824 | tf_op jit(solution)/shard_map/dot_general | solution.py:139
  176.6 0.0 reduce-scatter.2.cloned.1.call-update
  176.6 47.3 %reduce-scatter.2.cloned.1.call-done = bf16[256,512]{1,0:T(8,128)(2,1)} async-done(((bf16[256,4096]{1,0:T(8,128)(2,1)}), bf16[256,512]{1,0:T(8,128)(2,1)}) %reduce-scatter.2.cloned.1.call-update) | async-done | bytes 262160 | tf_op jit(solution)/shard_map/reduce_scatter | solution.py:145
  (18 shorter events, 0.2 us)
Async XLA Ops:
  6.5 164.1 %all-gather.2.cloned.1.call-start = ((), (), s32[]{:S(2)}) async-start(), calls=%async_computation.1 | async-start | bytes 6389760 | tf_op jit(solution)/shard_map/all_gather | solution.py:141
  8.1 19.6 %copy-start = (bf16[256,128]{1,0:T(8,128)(2,1)S(1)}, bf16[256,128]{1,0:T(8,128)(2,1)}, u32[]{:S(2)}) copy-start(bf16[256,128]{1,0:T(8,128)(2,1)} %param.11) | copy-start | bytes 196612
  8.1 215.8 %reduce-scatter.2.cloned.1.call-start = ((), (), s32[]{:S(2)}) async-start(), calls=%async_computation.2 | async-start | bytes 2359296 | tf_op jit(solution)/shard_map/reduce_scatter | solution.py:145
  8.1 19.5 %collective-permute-start = (bf16[256,128]{1,0:T(8,128)(2,1)}, bf16[256,128]{1,0:T(8,128)(2,1)S(1)}, u32[]{:S(2)}, u32[]{:S(2)}) collective-permute-start(bf16[256,128]{1,0:T(8,128)(2,1)} %param.11), channel_id=1, source_target_pairs={{0,16},{8,24},{16,32},{24,40},{32,48},{40,56},{48,64},{56,72},{64,... | collective-permute-start | bytes 196616 | tf_op jit(solution)/shard_map/ppermute | solution.py:13
  11.9 15.7 %collective-permute-start.1 = (bf16[256,128]{1,0:T(8,128)(2,1)}, bf16[256,128]{1,0:T(8,128)(2,1)S(1)}, u32[]{:S(2)}, u32[]{:S(2)}) collective-permute-start(bf16[256,128]{1,0:T(8,128)(2,1)} %param.11), channel_id=1, source_target_pairs={{0,8},{8,16},{16,24},{24,32},{32,40},{40,48},{48,56},{56,64},{64,7... | collective-permute-start | bytes 196616 | tf_op jit(solution)/shard_map/ppermute | solution.py:13
  13.8 14.6 %collective-permute-start.2 = (bf16[256,128]{1,0:T(8,128)(2,1)}, bf16[256,128]{1,0:T(8,128)(2,1)S(1)}, u32[]{:S(2)}, u32[]{:S(2)}) collective-permute-start(bf16[256,128]{1,0:T(8,128)(2,1)} %param.12), channel_id=1, source_target_pairs={{0,16},{8,24},{16,32},{24,40},{32,48},{40,56},{48,64},{56,72},{64,... | collective-permute-start | bytes 196616 | tf_op jit(solution)/shard_map/ppermute | solution.py:13
  18.8 9.6 %collective-permute-start.3 = (bf16[256,128]{1,0:T(8,128)(2,1)}, bf16[256,128]{1,0:T(8,128)(2,1)S(1)}, u32[]{:S(2)}, u32[]{:S(2)}) collective-permute-start(bf16[256,128]{1,0:T(8,128)(2,1)} %param.12), channel_id=1, source_target_pairs={{0,8},{8,16},{16,24},{24,32},{32,40},{40,48},{48,56},{56,64},{64,7... | collective-permute-start | bytes 196616 | tf_op jit(solution)/shard_map/ppermute | solution.py:13
  26.8 1.6 copy-start.1
  27.6 1.6 copy-start.2
  34.3 13.9 %collective-permute-start.4 = (f32[2,128,128]{2,0,1:T(2,128)S(1)}, f32[2,128,128]{2,0,1:T(2,128)S(1)}, u32[]{:S(2)}, u32[]{:S(2)}) collective-permute-start(f32[2,128,128]{2,0,1:T(2,128)S(1)} %get-tuple-element.7), channel_id=1, source_target_pairs={{8,0},{16,8},{24,16},{32,24},{40,32},{48,40},{56,48},{64,56},{72,6... | collective-permute-start | bytes 393224 | tf_op jit(solution)/shard_map/ppermute | solution.py:13
  37.8 10.4 %collective-permute-start.5 = (f32[2,128,128]{2,0,1:T(2,128)S(1)}, f32[2,128,128]{2,0,1:T(2,128)S(1)}, u32[]{:S(2)}, u32[]{:S(2)}) collective-permute-start(f32[2,128,128]{2,0,1:T(2,128)S(1)} %get-tuple-element.8), channel_id=1, source_target_pairs={{16,0},{24,8},{32,16},{40,24},{48,32},{56,40},{64,48},{72,56},{80,... | collective-permute-start | bytes 393224 | tf_op jit(solution)/shard_map/ppermute | solution.py:13
  44.0 4.4 %collective-permute-start.6 = (f32[2,128,128]{2,0,1:T(2,128)S(1)}, f32[2,128,128]{2,0,1:T(2,128)S(1)}, u32[]{:S(2)}, u32[]{:S(2)}) collective-permute-start(f32[2,128,128]{2,0,1:T(2,128)S(1)} %get-tuple-element.9), channel_id=1, source_target_pairs={{8,0},{16,8},{24,16},{32,24},{40,32},{48,40},{56,48},{64,56},{72,6... | collective-permute-start | bytes 393224 | tf_op jit(solution)/shard_map/ppermute | solution.py:13
  46.0 11.1 %collective-permute-start.7 = (f32[2,128,128]{2,0,1:T(2,128)S(1)}, f32[2,128,128]{2,0,1:T(2,128)S(1)}, u32[]{:S(2)}, u32[]{:S(2)}) collective-permute-start(f32[2,128,128]{2,0,1:T(2,128)S(1)} %get-tuple-element.10), channel_id=1, source_target_pairs={{16,0},{24,8},{32,16},{40,24},{48,32},{56,40},{64,48},{72,56},{80,... | collective-permute-start | bytes 393224 | tf_op jit(solution)/shard_map/ppermute | solution.py:13
Sparse Core Ops, SparseCore 0:
  10.6 159.9 all-gather.1
  176.7 47.1 reduce-scatter.1
where the time goes:
time: 231 us
  waiting for transfers between devices  169 us (73%)
  starting transfers between devices  23.5 us (10%)
  matrix products  15.1 us (7%)
  between operations  13.7 us (6%)
  local copies, waits for them, and re-layouts  4.78 us (2%)
  other arithmetic  4.14 us (2%)
    all_gather x1, waiting for transfers between devices, per_device(): lax.all_gather(weight_cat, 'ctx', axis=0, tiled=True)  113 us
    reduce_scatter x1, waiting for transfers between devices, per_device(): lax.psum_scatter(partial_value.astype(jnp.bfloat16), 'head', scatter_dime...  47.3 us
    ppermute x8, starting transfers between devices, passed_along(): return lax.ppermute(x, axis, pairs)  23.5 us
    ppermute x8, waiting for transfers between devices, passed_along(): return lax.ppermute(x, axis, pairs)  8.79 us
    dot_general x1, matrix products, per_device(): lax.dot_general(grads, lax.all_gather(weight_cat, 'ctx', axis=0, tiled=Tr...  5.96 us
  transfers between devices with their start and end apart: 10, of which 4 were waited for; matrix products, arithmetic and copies ran while one was open for 7% of the time, Pallas kernels for 0%

commit v1 on v0

--- a/solution.py
+++ b/solution.py
@@ -138,7 +138,9 @@
     weight_cat = jnp.concatenate([query_weight, key_weight, value_weight], axis=1)
     partial_value = lax.dot_general(
         grads,
-        lax.all_gather(weight_cat, "ctx", axis=0, tiled=True),
+        jnp.concatenate(
+            lax.all_to_all(jnp.stack([weight_cat] * lax.axis_size("ctx")), "ctx", 0, 0), axis=0
+        ),
         (((1,), (1,)), ((), ())),
         preferred_element_type=jnp.float32,
     )

time: 231 us -> 401 us (1.74)
  waiting for transfers between devices: 169 us -> 316 us
  starting transfers between devices: 23.5 us -> 40 us
    ppermute x8, waiting for transfers between devices: 8.79 us -> 258 us  [passed_along(): return lax.ppermute(x, axis, pairs)]
    all_gather x1 -> x0, waiting for transfers between devices: 113 us -> none  [per_device(): lax.all_gather(weight_cat, 'ctx', axis=0, tiled=True)]
    all_to_all x0 -> x1, starting transfers between devices: none -> 18.9 us  [per_device(): lax.all_to_all(jnp.stack([weight_cat] * lax.axis_size('ctx')), 'ctx', 0, 0)]
    reduce_scatter x1, waiting for transfers between devices: 47.3 us -> 57.7 us  [per_device(): lax.psum_scatter(partial_value.astype(jnp.bfloat16), 'head', scatter_dime...]
  transfers between devices with their start and end apart: 10 -> 10, of which waited for: 4 -> 3; matrix products, arithmetic and copies ran while one was open for 7% -> 5% of each run, Pallas kernels for 0% -> 0%
where the time goes in v1:
time: 401 us; the launch traced here: 400 us
  waiting for transfers between devices  316 us (79%)
  starting transfers between devices  40 us (10%)
  matrix products  17.3 us (4%)
  between operations  13.8 us (3%)
  local copies, waits for them, and re-layouts  8.38 us (2%)
  other arithmetic  4.37 us (1%)
    ppermute x8, waiting for transfers between devices, passed_along(): return lax.ppermute(x, axis, pairs)  258 us
    reduce_scatter x1, waiting for transfers between devices, per_device(): lax.psum_scatter(partial_value.astype(jnp.bfloat16), 'head', scatter_dime...  57.7 us
    ppermute x8, starting transfers between devices, passed_along(): return lax.ppermute(x, axis, pairs)  21 us
    all_to_all x1, starting transfers between devices, per_device(): lax.all_to_all(jnp.stack([weight_cat] * lax.axis_size('ctx')), 'ctx', 0, 0)  18.9 us
  transfers between devices with their start and end apart: 10, of which 3 were waited for; matrix products, arithmetic and copies ran while one was open for 5% of the time, Pallas kernels for 0%

profile of v1, /device:TPU:4, one launch (start us, length us, event | category | flops | bytes accessed | tf_op | source)
XLA Modules:
  0.0 400.0 jit_solution(10323380798773277134)
XLA Ops:
  6.5 0.9 pad_maximum_fusion.2
  7.4 3.4 stack.2
  10.8 0.0 copy-start.4
  10.8 0.0 copy-start.7
  10.8 18.9 %all-to-all-start = ((bf16[64,64,768]{2,1,0:T(8,128)(2,1)}), bf16[64,64,768]{2,1,0:T(8,128)(2,1)}, u32[]{:S(2)}, u32[]{:S(2)}) async-start(bf16[64,64,768]{2,1,0:T(8,128)(2,1)} %stack.2), calls=%async_computation | async-start | bytes 12582912 | tf_op jit(solution)/shard_map/all_to_all | solution.py:142
  29.8 0.0 reduce-scatter.2.cloned.1.call-start
  29.8 2.0 collective-permute-start.1
  31.8 3.4 collective-permute-start
  35.2 4.6 %collective-permute-start.3 = (bf16[256,128]{1,0:T(8,128)(2,1)S(1)}, bf16[256,128]{1,0:T(8,128)(2,1)}, u32[]{:S(2)}, u32[]{:S(2)}) collective-permute-start(bf16[256,128]{1,0:T(8,128)(2,1)S(1)} %copy-done.9), channel_id=1, source_target_pairs={{0,8},{8,16},{16,24},{24,32},{32,40},{40,48},{48,56},{56,64},{64,7... | collective-permute-start | bytes 196616 | tf_op jit(solution)/shard_map/ppermute | solution.py:13
  39.8 3.4 collective-permute-start.2
  43.3 0.1 compare_select_fusion
  43.3 0.1 copy.38
  43.4 0.1 reshape.60
  43.5 0.1 compare_and_fusion
  43.6 0.7 copy.41
  44.3 0.1 copy.40
  44.4 0.8 reshape.52
  45.2 0.1 reshape.55
  45.3 0.1 copy.50
  45.4 0.1 convert_multiply_fusion
  45.4 0.2 reshape.56
  45.6 0.3 reduce_sum.9
  46.0 0.1 copy.46
  46.1 0.6 iota_compare_fusion
  46.7 252.0 %collective-permute-done = bf16[256,128]{1,0:T(8,128)(2,1)S(1)} collective-permute-done((bf16[256,128]{1,0:T(8,128)(2,1)S(1)}, bf16[256,128]{1,0:T(8,128)(2,1)S(1)}, u32[]{:S(2)}, u32[]{:S(2)}) %collective-permute-start) | collective-permute-done | bytes 65568 | tf_op jit(solution)/shard_map/ppermute | solution.py:13
  298.7 0.7 gather_fusion
  299.5 1.9 bitcast_select_fusion
  301.5 0.4 fusion.14
  301.9 3.3 fusion.8
  305.2 0.9 fusion.35
  306.1 1.9 collective-permute-start.7
  308.0 1.9 collective-permute-start.6
  310.0 0.9 pad_maximum_fusion.1
  310.9 0.7 gather_fusion.1
  311.6 1.4 fusion
  313.1 0.4 convolution_multiply_fusion
  313.5 3.3 fusion.5
  316.8 0.5 fusion.13
  317.3 0.1 fusion.34
  317.4 1.9 collective-permute-start.5
  319.3 1.9 collective-permute-start.4
  321.2 0.2 copy.48
  321.5 1.2 fusion.26
  322.8 6.4 %collective-permute-done.5 = f32[2,128,128]{2,0,1:T(2,128)S(1)} collective-permute-done((f32[2,128,128]{2,0,1:T(2,128)S(1)}, f32[2,128,128]{2,0,1:T(2,128)S(1)}, u32[]{:S(2)}, u32[]{:S(2)}) %collective-permute-start.5) | collective-permute-done | bytes 131104 | tf_op jit(solution)/shard_map/ppermute | solution.py:13
  329.2 0.1 fusion.28
  329.4 6.0 %convolution_convert_fusion = bf16[256,4096]{1,0:T(8,128)(2,1)} fusion(bf16[4096,768]{1,0:T(8,128)(2,1)} %bitcast.28, bf16[256,128]{1,0:T(8,128)(2,1)S(1)} %bitcast.71, bf16[256,128]{1,0:T(8,128)(2,1)S(1)} %bitcast.72, bf16[256,512]{1,0:T(8,128)(2,1)S(1)} %bitcast.70), kind=kOutput, calls=%fused_computation.2 | convolution fusion | flops 1612840960 | bytes 8781824 | tf_op jit(solution)/shard_map/dot_general | solution.py:139
  335.4 0.0 reduce-scatter.2.cloned.1.call-update
  335.4 57.7 %reduce-scatter.2.cloned.1.call-done = bf16[256,512]{1,0:T(8,128)(2,1)} async-done(((bf16[256,4096]{1,0:T(8,128)(2,1)}), bf16[256,512]{1,0:T(8,128)(2,1)}) %reduce-scatter.2.cloned.1.call-update) | async-done | bytes 262160 | tf_op jit(solution)/shard_map/reduce_scatter | solution.py:147
  (36 shorter events, 0.2 us)
Async XLA Ops:
  10.8 19.0 %copy-start.8 = (bf16[256,128]{1,0:T(8,128)(2,1)S(1)}, bf16[256,128]{1,0:T(8,128)(2,1)}, u32[]{:S(2)}) copy-start(bf16[256,128]{1,0:T(8,128)(2,1)} %param.11) | copy-start | bytes 196612
  10.8 24.4 %copy-start.9 = (bf16[256,128]{1,0:T(8,128)(2,1)S(1)}, bf16[256,128]{1,0:T(8,128)(2,1)}, u32[]{:S(2)}) copy-start(bf16[256,128]{1,0:T(8,128)(2,1)} %param.12) | copy-start | bytes 196612
  10.8 32.4 %copy-start.11 = (s32[2,4,3]{1,0,2:T(2,128)S(1)}, s32[2,4,3]{1,0,2:T(2,128)}, u32[]{:S(2)}) copy-start(s32[2,4,3]{1,0,2:T(2,128)} %param.16) | copy-start | bytes 292
  10.8 33.6 %copy-start.6 = (bf16[256,512]{1,0:T(8,128)(2,1)S(1)}, bf16[256,512]{1,0:T(8,128)(2,1)}, u32[]{:S(2)}) copy-start(bf16[256,512]{1,0:T(8,128)(2,1)} %param.10) | copy-start | bytes 786436
  10.8 34.4 %copy-start.4 = (bf16[256,512]{1,0:T(8,128)(2,1)S(1)}, bf16[256,512]{1,0:T(8,128)(2,1)}, u32[]{:S(2)}) copy-start(bf16[256,512]{1,0:T(8,128)(2,1)} %param.14) | copy-start | bytes 786436
  10.8 34.6 %copy-start.7 = (bf16[256,512]{1,0:T(8,128)(2,1)S(1)}, bf16[256,512]{1,0:T(8,128)(2,1)}, u32[]{:S(2)}) copy-start(bf16[256,512]{1,0:T(8,128)(2,1)} %param.13) | copy-start | bytes 786436
  10.8 318.6 %all-to-all-start = ((bf16[64,64,768]{2,1,0:T(8,128)(2,1)}), bf16[64,64,768]{2,1,0:T(8,128)(2,1)}, u32[]{:S(2)}, u32[]{:S(2)}) async-start(bf16[64,64,768]{2,1,0:T(8,128)(2,1)} %stack.2), calls=%async_computation | async-start | bytes 12582912 | tf_op jit(solution)/shard_map/all_to_all | solution.py:142
  29.8 363.4 %reduce-scatter.2.cloned.1.call-start = ((), (), s32[]{:S(2)}) async-start(), calls=%async_computation.2 | async-start | bytes 2359296 | tf_op jit(solution)/shard_map/reduce_scatter | solution.py:147
  29.8 16.9 %collective-permute-start.1 = (bf16[256,128]{1,0:T(8,128)(2,1)S(1)}, bf16[256,128]{1,0:T(8,128)(2,1)S(1)}, u32[]{:S(2)}, u32[]{:S(2)}) collective-permute-start(bf16[256,128]{1,0:T(8,128)(2,1)S(1)} %copy-done.8), channel_id=1, source_target_pairs={{0,8},{8,16},{16,24},{24,32},{32,40},{40,48},{48,56},{56,64},{64,7... | collective-permute-start | bytes 196616 | tf_op jit(solution)/shard_map/ppermute | solution.py:13
  31.8 266.8 %collective-permute-start = (bf16[256,128]{1,0:T(8,128)(2,1)S(1)}, bf16[256,128]{1,0:T(8,128)(2,1)S(1)}, u32[]{:S(2)}, u32[]{:S(2)}) collective-permute-start(bf16[256,128]{1,0:T(8,128)(2,1)S(1)} %copy-done.8), channel_id=1, source_target_pairs={{0,16},{8,24},{16,32},{24,40},{32,48},{40,56},{48,64},{56,72},{64,... | collective-permute-start | bytes 196616 | tf_op jit(solution)/shard_map/ppermute | solution.py:13
  35.2 274.7 %collective-permute-start.3 = (bf16[256,128]{1,0:T(8,128)(2,1)S(1)}, bf16[256,128]{1,0:T(8,128)(2,1)}, u32[]{:S(2)}, u32[]{:S(2)}) collective-permute-start(bf16[256,128]{1,0:T(8,128)(2,1)S(1)} %copy-done.9), channel_id=1, source_target_pairs={{0,8},{8,16},{16,24},{24,32},{32,40},{40,48},{48,56},{56,64},{64,7... | collective-permute-start | bytes 196616 | tf_op jit(solution)/shard_map/ppermute | solution.py:13
  39.8 270.1 %collective-permute-start.2 = (bf16[256,128]{1,0:T(8,128)(2,1)S(1)}, bf16[256,128]{1,0:T(8,128)(2,1)}, u32[]{:S(2)}, u32[]{:S(2)}) collective-permute-start(bf16[256,128]{1,0:T(8,128)(2,1)S(1)} %copy-done.9), channel_id=1, source_target_pairs={{0,16},{8,24},{16,32},{24,40},{32,48},{40,56},{48,64},{56,72},{64,... | collective-permute-start | bytes 196616 | tf_op jit(solution)/shard_map/ppermute | solution.py:13
  45.3 256.2 %copy-start.2 = (bf16[2,128,4,128]{3,2,1,0:T(4,128)(2,1)}, bf16[2,128,4,128]{3,2,1,0:T(4,128)(2,1)S(1)}, u32[]{:S(2)}) copy-start(bf16[2,128,4,128]{3,2,1,0:T(4,128)(2,1)S(1)} %reshape.55) | copy-start | bytes 786436
  298.7 0.8 copy-start.10
  299.5 2.0 copy-start
  305.2 5.7 %copy-start.3 = (f32[6,128,128]{2,0,1:T(8,128)}, f32[6,128,128]{2,0,1:T(8,128)S(1)}, u32[]{:S(2)}) copy-start(f32[6,128,128]{2,0,1:T(8,128)S(1)} %fusion.8) | copy-start | bytes 1179652
  306.1 15.4 %collective-permute-start.7 = (f32[2,128,128]{2,0,1:T(2,128)}, f32[2,128,128]{2,0,1:T(2,128)S(1)}, u32[]{:S(2)}, u32[]{:S(2)}) collective-permute-start(f32[2,128,128]{2,0,1:T(2,128)} %get-tuple-element.10), channel_id=1, source_target_pairs={{16,0},{24,8},{32,16},{40,24},{48,32},{56,40},{64,48},{72,56},{80,... | collective-permute-start | bytes 393224 | tf_op jit(solution)/shard_map/ppermute | solution.py:13
  308.0 13.5 %collective-permute-start.6 = (f32[2,128,128]{2,0,1:T(2,128)}, f32[2,128,128]{2,0,1:T(2,128)}, u32[]{:S(2)}, u32[]{:S(2)}) collective-permute-start(f32[2,128,128]{2,0,1:T(2,128)} %get-tuple-element.9), channel_id=1, source_target_pairs={{8,0},{16,8},{24,16},{32,24},{40,32},{48,40},{56,48},{64,56},{72,6... | collective-permute-start | bytes 393224 | tf_op jit(solution)/shard_map/ppermute | solution.py:13
  311.6 1.4 copy-start.5
  313.5 3.3 copy-start.1
  317.4 11.8 %collective-permute-start.5 = (f32[2,128,128]{2,0,1:T(2,128)S(1)}, f32[2,128,128]{2,0,1:T(2,128)S(1)}, u32[]{:S(2)}, u32[]{:S(2)}) collective-permute-start(f32[2,128,128]{2,0,1:T(2,128)S(1)} %get-tuple-element.8), channel_id=1, source_target_pairs={{16,0},{24,8},{32,16},{40,24},{48,32},{56,40},{64,48},{72,56},{80,... | collective-permute-start | bytes 393224 | tf_op jit(solution)/shard_map/ppermute | solution.py:13
  319.3 9.9 %collective-permute-start.4 = (f32[2,128,128]{2,0,1:T(2,128)S(1)}, f32[2,128,128]{2,0,1:T(2,128)S(1)}, u32[]{:S(2)}, u32[]{:S(2)}) collective-permute-start(f32[2,128,128]{2,0,1:T(2,128)S(1)} %get-tuple-element.7), channel_id=1, source_target_pairs={{8,0},{16,8},{24,16},{32,24},{40,32},{48,40},{56,48},{64,56},{72,6... | collective-permute-start | bytes 393224 | tf_op jit(solution)/shard_map/ppermute | solution.py:13
Sparse Core Ops, SparseCore 0:
  335.5 57.5 reduce-scatter.1
